TPU v7x, 32 devices: a whole 2x2x4 slice. The times are simulated.
32 devices in a mesh: dp: 4 (over x, core), cls: 8 (over z, y).
Axes of the slice: x: 2, y: 2, z: 4, core: 2. Of those that a mesh axis runs over, the one named last changes fastest.
Arguments:
- pooled: bfloat16 [4096, 512], P(('dp', 'cls')), may hold values from -6 to 6
- proj: bfloat16 [512, 512], replicated, may hold values from -0.25 to 0.25
- centers: bfloat16 [2048, 512], P('cls'), may hold values from -6 to 6
- labels: int32 [4096], P(('dp', 'cls')), may hold values from 0 to 2047
- row_weight: bfloat16 [4096], P(('dp', 'cls')), may hold values from 0.5 to 2
Outputs:
- row_loss: float32 [4096], P(('dp', 'cls'))
- center_grad: float32 [2048, 512], P('cls')
- proj_grad: float32 [512, 512], replicated
All inputs are finite; a program needn't handle non-finite values.
Results may differ from a plain program's by a relative error of at most 0.005.
Values may be sent and summed in bfloat16 or wider, within the bound.
No kernel may reach another device: no remote copies, remote signals or barrier semaphores. Data moves between devices by JAX's collectives and lax.ppermute only.
A program may use at most 128 MiB of HBM per device.

v0:
```python
import math
import jax
import jax.numpy as jnp
from jax import lax
from jax.sharding import PartitionSpec as P

SCALE = 64.0
MARGIN = 0.35
EPS = 1e-06


def unit_rows(values):
    inverse = lax.rsqrt(jnp.sum(values * values, axis=1, keepdims=True) + EPS)
    return ((values * inverse).astype(jnp.bfloat16), inverse)


def onehot_of(lab_block, width):
    columns = jnp.arange(width, dtype=jnp.int32)
    return (lab_block[:, None] == columns[None, :]).astype(jnp.float32)


def split_product(feat_rows, grad_hidden):
    upper = grad_hidden.astype(jnp.bfloat16)
    lower = (grad_hidden - upper.astype(jnp.float32)).astype(jnp.bfloat16)
    dims = (((0,), (0,)), ((), ()))
    first = lax.dot_general(feat_rows, upper, dims, preferred_element_type=jnp.float32)
    second = lax.dot_general(feat_rows, lower, dims, preferred_element_type=jnp.float32)
    return first + second


def on_device(pooled, proj, centers, labels, row_weight):
    rows = pooled.shape[0]
    c_dev = centers.shape[0]
    width = centers.shape[1]
    shard = lax.axis_index("cls")
    unit, c_inv = unit_rows(centers.astype(jnp.float32))
    label_all = lax.all_gather(labels, "cls", axis=0, tiled=True) - shard * c_dev
    feat_all, weight_all = (
        lax.all_gather(pooled, "cls", axis=0, tiled=True),
        lax.all_gather(row_weight, "cls", axis=0, tiled=True),
    )
    hidden = jnp.dot(feat_all, proj, preferred_element_type=jnp.float32)
    emb_all, z_inv = unit_rows(hidden)
    total_rows = emb_all.shape[0]
    block = math.gcd(total_rows, 1024)
    count = total_rows // block
    emb_blocks = emb_all.reshape(count, block, width)
    lab_blocks = label_all.reshape(count, block)

    def stats_step(carry, pieces):
        emb_block, lab_block = pieces
        cosine = lax.dot_general(
            emb_block, unit, (((1,), (1,)), ((), ())), preferred_element_type=jnp.float32
        )
        onehot = onehot_of(lab_block, c_dev)
        logits = SCALE * cosine - SCALE * MARGIN * onehot
        expo = jnp.exp(logits)
        return (carry, (expo, jnp.sum(expo, axis=1), jnp.sum(logits * onehot, axis=1)))

    _, (expo_blocks, part_total, part_target) = lax.scan(
        stats_step, jnp.zeros((), jnp.float32), (emb_blocks, lab_blocks)
    )
    total, target = lax.psum(
        (part_total.reshape(total_rows), part_target.reshape(total_rows)), "cls"
    )
    loss_all = jnp.log(total) - target

    def grad_step(accum, pieces):
        emb_block, lab_block, expo_block, total_block, weight_block = pieces
        onehot = onehot_of(lab_block, c_dev)
        grad_block = (weight_block[:, None] * (expo_block / total_block[:, None] - onehot)).astype(
            jnp.bfloat16
        )
        accum = accum + SCALE * lax.dot_general(
            grad_block, emb_block, (((0,), (0,)), ((), ())), preferred_element_type=jnp.float32
        )
        return (accum, grad_block)

    grad_unit, grad_blocks = lax.scan(
        grad_step,
        jnp.zeros((c_dev, width), jnp.float32),
        (
            emb_blocks,
            lab_blocks,
            expo_blocks,
            total.reshape(count, block),
            weight_all.astype(jnp.float32).reshape(count, block),
        ),
    )
    grad_logits = grad_blocks.reshape(total_rows, c_dev)
    grad_unit = lax.psum(grad_unit, "dp")
    unit_f = unit.astype(jnp.float32)
    center_grad = c_inv * (grad_unit - unit_f * jnp.sum(unit_f * grad_unit, axis=1, keepdims=True))
    grad_emb = SCALE * jnp.dot(grad_logits, unit, preferred_element_type=jnp.float32)
    row_loss = lax.dynamic_slice_in_dim(loss_all, shard * rows, rows)
    emb_f = emb_all.astype(jnp.float32)
    grad_hidden = z_inv * (grad_emb - emb_f * jnp.sum(emb_f * grad_emb, axis=1, keepdims=True))
    proj_part = split_product(feat_all, grad_hidden)
    proj_grad = lax.psum(proj_part, ("dp", "cls"))
    return (row_loss, center_grad, proj_grad)


def solution(mesh):
    in_specs = (P(("dp", "cls"), None), P(), P("cls", None), P(("dp", "cls")), P(("dp", "cls")))
    out_specs = (P(("dp", "cls")), P("cls", None), P())
    return jax.shard_map(
        on_device, mesh=mesh, in_specs=in_specs, out_specs=out_specs, check_vma=False
    )
```

profile of v0, /device:TPU:0, one launch (start us, length us, event | category | flops | bytes accessed | tf_op | source)
XLA Modules:
  0.0 259.5 jit_solution(14060492183931136996)
XLA Ops:
  7.2 0.0 copy-start
  7.2 0.0 all-gather.4.cloned.1.call-start
  7.2 0.7 all-gather.4.cloned.1.call-update
  7.9 0.0 all-reduce.4.cloned.1.call-start
  8.0 22.5 %all-gather.1 = bf16[8,1,128]{2,1,0:T(2,128)(2,1)S(1)} all-gather(bf16[1,1,128]{2,1,0:T(2,128)(2,1)} %bitcast.20), channel_id=1, replica_groups=mesh['dp'=4,'cls'=8] {'cls'}, dimensions={0}, use_global_device_ids=true | all-gather | bytes 2304 | tf_op jit(solution)/shard_map/all_gather | solution.py:40
  30.4 16.6 %all-gather = s32[8,1,128]{2,1,0:T(1,128)S(1)} all-gather(s32[1,1,128]{2,1,0:T(1,128)} %bitcast.21), channel_id=1, replica_groups=mesh['dp'=4,'cls'=8] {'cls'}, dimensions={0}, use_global_device_ids=true | all-gather | bytes 4608 | tf_op jit(solution)/shard_map/all_gather | solution.py:37
  47.0 1.1 fusion.14
  48.2 5.0 %all-gather.4.cloned.1.call-done = bf16[1024,512]{1,0:T(8,128)(2,1)} async-done(((bf16[128,512]{1,0:T(8,128)(2,1)}), bf16[1024,512]{1,0:T(8,128)(2,1)}) %all-gather.4.cloned.1.call-update) | async-done | bytes 1048592 | tf_op jit(solution)/shard_map/all_gather | solution.py:39
  53.1 0.0 copy-done
  53.1 2.0 multiply_reduce_fusion
  55.1 0.0 copy-start.3
  55.1 0.3 multiply_convert_fusion
  55.4 0.7 copy-done.3
  56.1 1.6 exponential_reduce_fusion
  57.7 19.4 %all-reduce = (f32[1024]{0:T(1024)S(1)}, f32[1024]{0:T(1024)S(1)}) all-reduce(f32[1024]{0:T(1024)S(1)} %get-tuple-element.47, f32[1024]{0:T(1024)S(1)} %get-tuple-element.46), channel_id=1, replica_groups=mesh['dp'=4,'cls'=8] {'cls'}, use_global_device_ids=true, to_apply=%region_5.6 | all-reduce | flops 2048 | bytes 16384 | tf_op jit(solution)/shard_map/psum | solution.py:63
  77.1 2.5 convolution_multiply_fusion.1
  79.6 0.0 copy-start.1
  79.6 3.3 %fusion = (f32[1024]{0:T(1024)S(1)}, f32[1024,512]{0,1:T(8,128)}) fusion(bf16[1024,512]{0,1:T(8,128)(2,1)S(1)} %multiply_convert_fusion, bf16[256,512]{1,0:T(8,128)(2,1)S(1)} %copy-done.3, f32[256]{0:T(256)S(1)} %add_rsqrt_fusion.1, f32[1024,256]{0,1:T(8,128)} %get-tuple-element.60, f32[1024]{0:T(1024)S(1)} %get-tuple-element.49, f32[1024]{0:T(1024)S(1)} %bitcast.16, ...), kind=kOutput, calls=%fused_computation.2 | convolution fusion | flops 272497664 | bytes 4473856 | tf_op jit(solution)/shard_map/dot_general | solution.py:94
  82.9 0.0 all-reduce.4.cloned.1.call-update
  83.0 0.0 all-reduce.6.cloned.1.call-start
  83.0 0.0 copy-done.1
  83.0 0.0 copy-start.2
  83.0 2.5 fusion.6
  85.5 0.0 copy-done.2
  85.5 1.7 fusion.3
  87.3 0.0 all-reduce.6.cloned.1.call-update
  87.3 0.6 dynamic_slice.21
  87.9 25.9 %all-reduce.4.cloned.1.call-done = f32[256,512]{1,0:T(8,128)} async-done(((f32[256,512]{1,0:T(8,128)}), f32[256,512]{1,0:T(8,128)}) %all-reduce.4.cloned.1.call-update) | async-done | bytes 524304 | tf_op jit(solution)/shard_map/psum | solution.py:91
  113.7 1.2 fusion.16
  115.0 2.0 fusion.18
  117.0 133.4 %all-reduce.6.cloned.1.call-done = f32[512,512]{0,1:T(8,128)} async-done(((f32[512,512]{0,1:T(8,128)}), f32[512,512]{0,1:T(8,128)}) %all-reduce.6.cloned.1.call-update) | async-done | bytes 1048592 | tf_op jit(solution)/shard_map/psum | solution.py:99
  250.4 2.5 copy.9
  (5 shorter events, 0.0 us)
Async XLA Ops:
  7.2 46.0 %copy-start = (bf16[512,512]{1,0:T(8,128)(2,1)S(1)}, bf16[512,512]{1,0:T(8,128)(2,1)}, u32[]{:S(2)}) copy-start(bf16[512,512]{1,0:T(8,128)(2,1)} %param.6) | copy-start | bytes 1572868
  7.2 45.9 %all-gather.4.cloned.1.call-start = ((), (), s32[]{:S(2)}) async-start(), calls=%async_computation | async-start | bytes 1179648 | tf_op jit(solution)/shard_map/all_gather | solution.py:39
  7.9 105.8 %all-reduce.4.cloned.1.call-start = ((), (), s32[]{:S(2)}) async-start(), calls=%async_computation.1 | async-start | bytes 1048576 | tf_op jit(solution)/shard_map/psum | solution.py:91
  55.1 1.0 copy-start.3
  79.6 3.4 %copy-start.1 = (bf16[1024,512]{1,0:T(8,128)(2,1)S(1)}, bf16[1024,512]{1,0:T(8,128)(2,1)}, u32[]{:S(2)}) copy-start(bf16[1024,512]{1,0:T(8,128)(2,1)} %all-gather.4.cloned.1.call-done) | copy-start | bytes 3145732
  83.0 167.4 %all-reduce.6.cloned.1.call-start = ((), (), s32[]{:S(2)}) async-start(), calls=%async_computation.2 | async-start | bytes 2097152 | tf_op jit(solution)/shard_map/psum | solution.py:99
  83.0 2.5 copy-start.2
Sparse Core Ops, SparseCore 0:
  10.1 42.9 all-gather.3
  83.1 30.5 all-reduce.3
  119.5 130.8 all-reduce.5
where the time goes:
time: 260 us; the launch traced here: 259 us
  waiting for transfers between devices  165 us (63%)
  blocking collectives  58.4 us (22%)
  between operations  13.8 us (5%)
  matrix products  13.7 us (5%)
  other arithmetic  4.62 us (2%)
  local copies, waits for them, and re-layouts  3.81 us (1%)
    psum x1, waiting for transfers between devices, on_device(): proj_grad = lax.psum(proj_part, ('dp', 'cls'))  133 us
    psum x1, waiting for transfers between devices, on_device(): grad_unit = lax.psum(grad_unit, 'dp')  25.9 us
    all_gather x1, blocking collectives, on_device(): lax.all_gather(row_weight, 'cls', axis=0, tiled=True)  22.5 us
    psum x1, blocking collectives, on_device(): lax.psum((part_total.reshape(total_rows), part_target.reshape(total_rows)...  19.4 us
    all_gather x1, blocking collectives, on_device(): lax.all_gather(labels, 'cls', axis=0, tiled=True) - shard * c_dev  16.6 us
  transfers between devices with their start and end apart: 3, of which 3 were waited for; matrix products, arithmetic and copies ran while one was open for 4% of the time, Pallas kernels for 0%

commit v1 on v0

--- a/solution.py
+++ b/solution.py
@@ -88,7 +88,7 @@
         ),
     )
     grad_logits = grad_blocks.reshape(total_rows, c_dev)
-    grad_unit = lax.psum(grad_unit, "dp")
+    grad_unit = lax.all_gather(grad_unit, axis_name="dp").sum(axis=0)
     unit_f = unit.astype(jnp.float32)
     center_grad = c_inv * (grad_unit - unit_f * jnp.sum(unit_f * grad_unit, axis=1, keepdims=True))
     grad_emb = SCALE * jnp.dot(grad_logits, unit, preferred_element_type=jnp.float32)

time: 260 us -> 242 us (0.931)
  waiting for transfers between devices: 165 us -> 153 us
  matrix products: 13.7 us -> 7.09 us
    psum x1 -> x0, waiting for transfers between devices: 25.9 us -> none  [on_device(): grad_unit = lax.psum(grad_unit, 'dp')]
    all_gather x0 -> x1, waiting for transfers between devices: none -> 21.2 us  [on_device(): grad_unit = lax.all_gather(grad_unit, axis_name='dp').sum(axis=0)]
    psum x1, waiting for transfers between devices: 133 us -> 126 us  [on_device(): proj_grad = lax.psum(proj_part, ('dp', 'cls'))]
    dot_general x1, matrix products: 3.33 us -> 0.68 us  [on_device(): jnp.dot(grad_logits, unit, preferred_element_type=jnp.float32)]
  transfers between devices with their start and end apart: 3 -> 3, of which waited for: 3 -> 3; matrix products, arithmetic and copies ran while one was open for 4% -> 2% of each run, Pallas kernels for 0% -> 0%
where the time goes in v1:
time: 242 us; the launch traced here: 241 us
  waiting for transfers between devices  153 us (63%)
  blocking collectives  58.5 us (24%)
  between operations  13.8 us (6%)
  matrix products  7.09 us (3%)
  other arithmetic  4.42 us (2%)
  local copies, waits for them, and re-layouts  4.33 us (2%)
    psum x1, waiting for transfers between devices, on_device(): proj_grad = lax.psum(proj_part, ('dp', 'cls'))  126 us
    all_gather x1, blocking collectives, on_device(): lax.all_gather(row_weight, 'cls', axis=0, tiled=True)  22.5 us
    all_gather x1, waiting for transfers between devices, on_device(): grad_unit = lax.all_gather(grad_unit, axis_name='dp').sum(axis=0)  21.2 us
    psum x1, blocking collectives, on_device(): lax.psum((part_total.reshape(total_rows), part_target.reshape(total_rows)...  19.4 us
    all_gather x1, blocking collectives, on_device(): lax.all_gather(labels, 'cls', axis=0, tiled=True) - shard * c_dev  16.6 us
    all_gather x1, waiting for transfers between devices, on_device(): lax.all_gather(pooled, 'cls', axis=0, tiled=True)  4.98 us
  transfers between devices with their start and end apart: 3, of which 3 were waited for; matrix products, arithmetic and copies ran while one was open for 2% of the time, Pallas kernels for 0%

profile of v1, /device:TPU:0, one launch (start us, length us, event | category | flops | bytes accessed | tf_op | source)
XLA Modules:
  0.0 241.2 jit_solution(9374848905410918199)
XLA Ops:
  7.2 0.0 copy-start
  7.2 0.0 all-gather.6.cloned.1.call-start
  7.2 0.7 all-gather.6.cloned.1.call-update
  7.9 0.0 all-reduce.3.cloned.1.call-start
  8.0 22.5 %all-gather.2 = bf16[8,1,128]{2,1,0:T(2,128)(2,1)S(1)} all-gather(bf16[1,1,128]{2,1,0:T(2,128)(2,1)} %bitcast.22), channel_id=1, replica_groups=mesh['dp'=4,'cls'=8] {'cls'}, dimensions={0}, use_global_device_ids=true | all-gather | bytes 2304 | tf_op jit(solution)/shard_map/all_gather | solution.py:40
  30.4 16.6 %all-gather.1 = s32[8,1,128]{2,1,0:T(1,128)S(1)} all-gather(s32[1,1,128]{2,1,0:T(1,128)} %bitcast.23), channel_id=1, replica_groups=mesh['dp'=4,'cls'=8] {'cls'}, dimensions={0}, use_global_device_ids=true | all-gather | bytes 4608 | tf_op jit(solution)/shard_map/all_gather | solution.py:37
  47.0 1.1 fusion.14
  48.2 5.0 %all-gather.6.cloned.1.call-done = bf16[1024,512]{1,0:T(8,128)(2,1)} async-done(((bf16[128,512]{1,0:T(8,128)(2,1)}), bf16[1024,512]{1,0:T(8,128)(2,1)}) %all-gather.6.cloned.1.call-update) | async-done | bytes 1048592 | tf_op jit(solution)/shard_map/all_gather | solution.py:39
  53.1 0.0 copy-done
  53.1 2.0 multiply_reduce_fusion
  55.1 0.0 copy-start.2
  55.2 0.3 multiply_convert_fusion
  55.4 0.7 copy-done.2
  56.1 0.7 exponential_reduce_fusion
  56.7 19.4 %all-reduce = (f32[1024]{0:T(1024)S(1)}, f32[1024]{0:T(1024)S(1)}) all-reduce(f32[1024]{0:T(1024)S(1)} %get-tuple-element.47, f32[1024]{0:T(1024)S(1)} %get-tuple-element.46), channel_id=1, replica_groups=mesh['dp'=4,'cls'=8] {'cls'}, use_global_device_ids=true, to_apply=%region_5.6 | all-reduce | flops 2048 | bytes 16384 | tf_op jit(solution)/shard_map/psum | solution.py:63
  76.2 0.0 copy-start.1
  76.2 0.7 fusion
  76.9 0.5 copy-done.1
  77.4 0.8 fusion.6
  78.2 1.7 fusion.3
  79.9 0.0 all-reduce.3.cloned.1.call-update
  79.9 0.0 all-gather.8.cloned.1.call-start
  79.9 1.3 convolution_multiply_fusion.1
  81.2 0.0 all-gather.8.cloned.1.call-update
  81.3 0.6 dynamic_slice.21
  81.9 126.0 %all-reduce.3.cloned.1.call-done = f32[512,512]{0,1:T(8,128)} async-done(((f32[512,512]{0,1:T(8,128)}), f32[512,512]{0,1:T(8,128)}) %all-reduce.3.cloned.1.call-update) | async-done | bytes 1048592 | tf_op jit(solution)/shard_map/psum | solution.py:99
  207.9 2.5 %copy.9 = f32[512,512]{1,0:T(8,128)} copy(f32[512,512]{0,1:T(8,128)} %all-reduce.3.cloned.1.call-done) | data formatting | bytes 2097152
  210.4 21.2 %all-gather.8.cloned.1.call-done = f32[1024,512]{1,0:T(8,128)} async-done(((f32[256,512]{1,0:T(8,128)}), f32[1024,512]{1,0:T(8,128)}) %all-gather.8.cloned.1.call-update) | async-done | bytes 2097168 | tf_op jit(solution)/shard_map/all_gather | solution.py:91
  231.6 1.9 reduce_sum.69
  233.4 0.2 fusion.16
  233.7 1.0 fusion.18
  (5 shorter events, 0.0 us)
Async XLA Ops:
  7.2 46.0 %copy-start = (bf16[512,512]{1,0:T(8,128)(2,1)S(1)}, bf16[512,512]{1,0:T(8,128)(2,1)}, u32[]{:S(2)}) copy-start(bf16[512,512]{1,0:T(8,128)(2,1)} %param.6) | copy-start | bytes 1572868
  7.2 46.0 %all-gather.6.cloned.1.call-start = ((), (), s32[]{:S(2)}) async-start(), calls=%async_computation | async-start | bytes 1179648 | tf_op jit(solution)/shard_map/all_gather | solution.py:39
  7.9 200.0 %all-reduce.3.cloned.1.call-start = ((), (), s32[]{:S(2)}) async-start(), calls=%async_computation.1 | async-start | bytes 2097152 | tf_op jit(solution)/shard_map/psum | solution.py:99
  55.1 1.0 copy-start.2
  76.2 1.2 copy-start.1
  79.9 151.7 %all-gather.8.cloned.1.call-start = ((), (), s32[]{:S(2)}) async-start(), calls=%async_computation.2 | async-start | bytes 2621440 | tf_op jit(solution)/shard_map/all_gather | solution.py:91
Sparse Core Ops, SparseCore 0:
  10.1 42.9 all-gather.5
  80.0 127.8 all-reduce.2
  210.0 21.4 all-gather.7
